TPU v7x, 32 devices: a whole 2x2x4 slice. The times are simulated.
32 devices in a mesh: parts: 2 (over x), lat: 8 (over z, y), lev: 2 (over core).
Axes of the slice: x: 2, y: 2, z: 4, core: 2. Of those that a mesh axis runs over, the one named last changes fastest.
Arguments:
- fields: float32 [5, 60, 128, 512], P(None, 'lev', ('parts', 'lat')), parts along dimension 2, may hold values from -6 to 6
- region: int32 [128, 512], P(('parts', 'lat')), parts along dimension 0, may hold values from 0 to 7
- land: int32 [128, 512], P(('parts', 'lat')), parts along dimension 0, may hold values 0 or 1
- coef_table: float32 [60, 8], replicated, may hold values from 0.02 to 0.24
- w_in: bfloat16 [1024, 300], replicated, may hold values from -0.375 to 0.375
- b_in: float32 [1024], replicated, may hold values from -3 to 3
- w_mid: bfloat16 [2, 1024, 1024], replicated, may hold values from -0.1875 to 0.1875
- b_mid: float32 [2, 1024], replicated, may hold values from -3 to 3
- w_out: bfloat16 [300, 1024], replicated, may hold values from -0.1875 to 0.1875
- b_out: float32 [300], replicated, may hold values from -3 to 3
Outputs:
- closure: float32 [5, 60, 128, 512], P(None, 'lev', ('parts', 'lat')), parts along dimension 2
There are 2 independent parts, one for each index of `parts`. A program takes and returns all parts, laid end to end along the dimension named above; an argument that names none is the same for every part. Nothing has to cross between parts.
All inputs are finite; a program needn't handle non-finite values. No bound on the sum of `land` on one device may be relied on, other than what follows from the above.
Results may differ from a plain program's by a relative error of at most 0.0025.
Values may be sent and summed in bfloat16 or wider, within the bound.
A program may use at most 64 MiB of HBM per device.

v0:
```python
import functools

import jax
import jax.numpy as jnp
from jax import lax
from jax.experimental import pallas as pl
from jax.experimental.pallas import tpu as pltpu
from jax.sharding import PartitionSpec as P

PRE = 4
POST = 2
MESH = pl.DeviceIdType.MESH
BF = jnp.bfloat16
F32 = jnp.float32


def gelu(x):
    scale = 0.7978845608028654
    inner = x * (scale + (scale * 0.044715) * (x * x))
    half = 0.5 * x
    return half + half * jnp.tanh(inner)


def kernel(
    n_lat, n_var, n_lev, n_row,
    region, land, table, bias, fields, w_in_hbm, w_mid_hbm, w_out_hbm,
    out,
    split, w_in, w_mid, w_out, wi, wo,
    sent, halo, marks, f0, f1, f2, f3, ef, nf, prof, other, h1, h2, flux_own, flux,
    in_sem, out_sem, w_sem, mark_send, mark_recv, halo_send, halo_recv, prof_send, prof_recv,
    flux_send, flux_recv, edge_send, edge_recv,
):
    lat = lax.axis_index("lat")
    lev = lax.axis_index("lev")
    peer = 1 - lev
    has_up = lat > 0
    has_down = lat < n_lat - 1
    pad_lev = table.shape[1]
    feat = n_var * pad_lev
    n_lon = out.shape[1]
    hid = w_mid.shape[1]
    n_mid = w_mid.shape[0]
    half = n_row // 2
    first = PRE
    last = PRE + n_row - 1

    lanes = split.shape[2]
    n_split = split.shape[0]

    def columns_of(ref, c):
        return ref.at[:, c * lanes : (c + 1) * lanes]

    pieces = [
        pltpu.make_async_copy(columns_of(fields, c), split.at[c], in_sem.at[c])
        for c in range(n_split)
    ]
    for piece in pieces:
        piece.start()
    loads = [
        pltpu.make_async_copy(w_in_hbm, w_in, w_sem.at[0]),
        pltpu.make_async_copy(w_out_hbm, w_out, w_sem.at[1]),
        pltpu.make_async_copy(w_mid_hbm, w_mid, w_sem.at[2]),
    ]
    for load in loads:
        load.start()

    barrier = pltpu.get_barrier_semaphore()
    pl.semaphore_signal(barrier, inc=1, device_id={"lev": peer}, device_id_type=MESH)

    @pl.when(has_up)
    def _():
        for j in range(2):
            pl.semaphore_signal(
                barrier, inc=1, device_id={"lat": lat - 1, "lev": j}, device_id_type=MESH
            )

    @pl.when(has_down)
    def _():
        for j in range(2):
            pl.semaphore_signal(
                barrier, inc=1, device_id={"lat": lat + 1, "lev": j}, device_id_type=MESH
            )

    def take_row(r):
        for v in range(n_var):
            base = v * n_lev * n_row
            values = jnp.concatenate(
                [split[c, pl.ds(base + r, n_lev, stride=n_row), :] for c in range(n_split)],
                axis=1,
            )
            values = jnp.concatenate(
                [values, jnp.zeros((pad_lev - n_lev, n_lon), F32)], axis=0
            )
            f0[PRE + r, v * pad_lev : (v + 1) * pad_lev, :] = values
            sent[r, v * pad_lev : (v + 1) * pad_lev, :] = values.astype(BF)

    def row_up(k):
        return pltpu.make_async_remote_copy(
            src_ref=sent.at[k], dst_ref=halo.at[1, k],
            send_sem=halo_send.at[1, k], recv_sem=halo_recv.at[1, k],
            device_id={"lat": lat - 1}, device_id_type=MESH,
        )

    def row_down(k):
        return pltpu.make_async_remote_copy(
            src_ref=sent.at[n_row - 1 - k], dst_ref=halo.at[0, k],
            send_sem=halo_send.at[0, k], recv_sem=halo_recv.at[0, k],
            device_id={"lat": lat + 1}, device_id_type=MESH,
        )

    def marks_to(side, which, source, target):
        return pltpu.make_async_remote_copy(
            src_ref=source, dst_ref=marks.at[side, which],
            send_sem=mark_send.at[side, which], recv_sem=mark_recv.at[side, which],
            device_id={"lat": target}, device_id_type=MESH,
        )

    for piece in pieces:
        piece.wait()
    take_row(0)
    take_row(n_row - 1)

    pl.semaphore_wait(barrier, 1 + 2 * has_up.astype(jnp.int32) + 2 * has_down.astype(jnp.int32))

    @pl.when(has_up)
    def _():
        marks_to(1, 0, region, lat - 1).start()
        marks_to(1, 1, land, lat - 1).start()
        row_up(0).start()

    @pl.when(has_down)
    def _():
        marks_to(0, 0, region, lat + 1).start()
        marks_to(0, 1, land, lat + 1).start()
        row_down(0).start()

    for k in range(1, PRE):
        take_row(k)
        take_row(n_row - 1 - k)

        @pl.when(has_up)
        def _():
            row_up(k).start()

        @pl.when(has_down)
        def _():
            row_down(k).start()

    columns = [
        jnp.broadcast_to(table[lev, :, k : k + 1], (pad_lev, n_lon))
        for k in range(table.shape[2])
    ]

    def coefficient(region_row, land_row):
        region_row = jnp.broadcast_to(region_row, (pad_lev, n_lon))
        total = columns[0]
        for k in range(1, len(columns)):
            total = jnp.where(region_row == k, columns[k], total)
        return total * (1.0 - 0.6 * land_row.astype(F32))

    for r in range(n_row):
        ef[first + r] = coefficient(region[r : r + 1, :], land[r : r + 1, :])

    def faces_north(i):
        nf[i] = jnp.sqrt(ef[i] * ef[i + 1])

    def faces_east(i):
        c = ef[i]
        ef[i] = jnp.sqrt(c * pltpu.roll(c, n_lon - 1, 1))

    for i in range(first, last):
        faces_north(i)

    def step_rows(src, dst, i, store=None):
        def body(v, carry):
            for s in range(0, pad_lev, 16):
                rows = pl.ds(pl.multiple_of(v * pad_lev + s, 16), 16)
                f = src[i, rows, :]
                east = ef[i, s : s + 16, :] * (pltpu.roll(f, n_lon - 1, 1) - f)
                zonal = east - pltpu.roll(east, 1, 1)
                north = nf[i, s : s + 16, :] * (src[i + 1, rows, :] - f)
                south = nf[i - 1, s : s + 16, :] * (f - src[i - 1, rows, :])
                value = f + zonal + (north - south)
                if store is None:
                    dst[i, rows, :] = value
                else:
                    store(v, s, rows, value)
            return carry

        lax.fori_loop(0, n_var, body, 0)

    def loop_rows(low, high, fn):
        def body(i, carry):
            fn(i)
            return carry

        lax.fori_loop(low, high, body, 0)

    for side in range(2):
        exists = has_up if side == 0 else has_down

        @pl.when(exists)
        def _():
            for which in range(2):
                marks_to(side, which, region, lat).wait_recv()
            for k in range(PRE):
                r = n_row - 1 - k if side == 0 else k
                i = first - 1 - k if side == 0 else last + 1 + k
                ef[i] = coefficient(
                    marks[side, 0, r : r + 1, :], marks[side, 1, r : r + 1, :]
                )

        @pl.when(jnp.logical_not(exists))
        def _():
            for k in range(PRE):
                i = first - 1 - k if side == 0 else last + 1 + k
                ef[i] = jnp.zeros((pad_lev, n_lon), F32)
                f0[i] = jnp.zeros((feat, n_lon), F32)

    for i in list(range(0, first)) + list(range(last, last + PRE)):
        faces_north(i)
    for i in range(0, last + PRE + 1):
        faces_east(i)

    loop_rows(first + 1, last, lambda i: step_rows(f0, f1, i))
    loop_rows(first + 2, last - 1, lambda i: step_rows(f1, f2, i))
    loop_rows(first + 3, last - 2, lambda i: step_rows(f2, f3, i))

    loads[0].wait()
    loads[1].wait()
    n_feat = w_in.shape[1]
    for j in range(2):
        f_id = lax.broadcasted_iota(jnp.int32, (n_feat, feat), 0)
        c_id = lax.broadcasted_iota(jnp.int32, (n_feat, feat), 1)
        l_id = c_id % pad_lev
        want = (c_id // pad_lev) * (2 * n_lev) + j * n_lev + l_id
        pick = jnp.where((f_id == want) & (l_id < n_lev), 1.0, 0.0).astype(BF)
        wi[j] = jnp.dot(w_in[...], pick, preferred_element_type=F32).astype(BF)
        f_id = lax.broadcasted_iota(jnp.int32, (feat, n_feat), 1)
        c_id = lax.broadcasted_iota(jnp.int32, (feat, n_feat), 0)
        l_id = c_id % pad_lev
        want = (c_id // pad_lev) * (2 * n_lev) + j * n_lev + l_id
        pick = jnp.where((f_id == want) & (l_id < n_lev), 1.0, 0.0).astype(BF)
        wo[j] = jnp.dot(pick, w_out[...], preferred_element_type=F32).astype(BF)
    loads[2].wait()

    tile = 256

    def with_bias(x, start, size):
        b = bias[start : start + size, :]
        return x + jnp.concatenate([b] * (n_lon // b.shape[1]), axis=1)

    def profile_copy(p):
        return pltpu.make_async_remote_copy(
            src_ref=prof.at[peer, p], dst_ref=other.at[p],
            send_sem=prof_send.at[p], recv_sem=prof_recv.at[p],
            device_id={"lev": peer}, device_id_type=MESH,
        )

    def flux_row(owner, p):
        return half - 1 - p + owner * (1 + 2 * p)

    def flux_copy(p):
        return pltpu.make_async_remote_copy(
            src_ref=flux_own.at[p, peer], dst_ref=flux.at[flux_row(lev, p) + POST],
            send_sem=flux_send.at[p], recv_sem=flux_recv.at[p],
            device_id={"lev": peer}, device_id_type=MESH,
        )

    def edge_copy(p, j):
        q = p - (half - POST)
        place = flux_row(lev, p) + POST + (1 - 2 * lev) * n_row
        return pltpu.make_async_remote_copy(
            src_ref=flux_own.at[p, j], dst_ref=flux.at[place],
            send_sem=edge_send.at[q, j], recv_sem=edge_recv.at[peer, q],
            device_id={"lat": lat - 1 + 2 * lev, "lev": j}, device_id_type=MESH,
        )

    has_edge = jnp.where(lev == 0, has_up, has_down)

    def phase(p, carry):
        for side in range(2):
            exists = has_up if side == 0 else has_down

            @pl.when(exists)
            def _():
                if side == 0:
                    row_down(p).wait_recv()
                    f0[first - 1 - p] = halo[0, p].astype(F32)
                else:
                    row_up(p).wait_recv()
                    f0[last + 1 + p] = halo[1, p].astype(F32)

        def save(side):
            def store(v, s, rows, value):
                prof[side, p, rows, :] = value.astype(BF)

            return store

        for side in range(2):
            at = lambda k: first - p + k if side == 0 else last + p - k
            step_rows(f0, f1, at(0))
            step_rows(f1, f2, at(1))
            step_rows(f2, f3, at(2))
            step_rows(f3, None, at(3), save(side))
        exchange = profile_copy(p)
        exchange.start()
        exchange.wait_recv()

        for m in range(0, hid, tile):
            x = jnp.dot(wi[lev, m : m + tile, :], prof[lev, p], preferred_element_type=F32)
            x = x + jnp.dot(
                wi[peer, m : m + tile, :], other[p], preferred_element_type=F32
            )
            h1[m : m + tile, :] = gelu(with_bias(x, m, tile)).astype(BF)
        now, then = h1, h2
        for layer in range(n_mid):
            for m in range(0, hid, tile):
                x = jnp.dot(w_mid[layer, m : m + tile, :], now[...], preferred_element_type=F32)
                x = with_bias(x, (layer + 1) * hid + m, tile)
                then[m : m + tile, :] = gelu(x).astype(BF)
            now, then = then, now
        for j in range(2):
            x = jnp.dot(wo[j], now[...], preferred_element_type=F32)
            flux_own[p, j] = with_bias(x, (n_mid + 1) * hid + j * feat, feat).astype(BF)
        flux[flux_row(lev, p) + POST] = flux_own[p, lev]
        flux_copy(p).start()

        @pl.when(has_edge & (p >= half - POST))
        def _():
            for j in range(2):
                edge_copy(p, j).start()

        return carry

    lax.fori_loop(0, PRE, phase, 0)

    for p in range(half):
        flux_copy(p).wait_recv()

    def widen(i):
        f0[i] = flux[i - PRE + POST].astype(F32)

    loop_rows(first, last + 1, widen)

    def finish(i):
        def store(v, s, rows, value):
            count = min(16, n_lev - s)
            base = v * (n_lev * n_row) + s * n_row + (i - first)
            for c in range(n_split):
                split[c, pl.ds(base, count, stride=n_row), :] = value[
                    :count, c * lanes : (c + 1) * lanes
                ]

        step_rows(f1, None, i, store)

    loop_rows(first + 1, last, lambda i: step_rows(f0, f1, i))
    loop_rows(first + 2, last - 1, finish)

    for side in range(2):
        exists = has_up if side == 0 else has_down

        @pl.when(exists)
        def _():
            for q in range(POST):
                pltpu.make_async_remote_copy(
                    src_ref=flux_own.at[0, 0], dst_ref=flux.at[0],
                    send_sem=edge_send.at[0, 0], recv_sem=edge_recv.at[side, q],
                    device_id={"lev": peer}, device_id_type=MESH,
                ).wait_recv()
            for q in range(POST):
                widen(first - 1 - q if side == 0 else last + 1 + q)

    for i in (first - 1, first, last, last + 1):
        step_rows(f0, f1, i)
    for i in (first, first + 1, last - 1, last):
        finish(i)
    results = [
        pltpu.make_async_copy(split.at[c], columns_of(out, c), out_sem.at[c])
        for c in range(n_split)
    ]
    for piece in results:
        piece.start()

    for k in range(PRE):
        profile_copy(k).wait_send()
        flux_copy(k).wait_send()

    @pl.when(has_up)
    def _():
        for which in range(2):
            marks_to(1, which, region, lat).wait_send()
        for k in range(PRE):
            row_up(k).wait_send()

    @pl.when(has_down)
    def _():
        for which in range(2):
            marks_to(0, which, region, lat).wait_send()
        for k in range(PRE):
            row_down(k).wait_send()

    @pl.when(has_edge)
    def _():
        for p in range(half - POST, half):
            for j in range(2):
                edge_copy(p, j).wait_send()

    for piece in results:
        piece.wait()


def per_device(n_lat, fields, region, land, coef_table, w_in, b_in, w_mid, b_mid, w_out, b_out):
    n_var, n_lev, n_row, n_lon = fields.shape
    hid = w_in.shape[0]
    pad_lev = -(-n_lev // 16) * 16
    extra = pad_lev - n_lev
    feat = n_var * pad_lev
    rows = n_row + 2 * PRE
    table = jnp.pad(coef_table.reshape(2, n_lev, -1), ((0, 0), (0, extra), (0, 0)))
    last_bias = jnp.pad(b_out.reshape(n_var, 2, n_lev), ((0, 0), (0, 0), (0, extra)))
    bias = jnp.concatenate(
        [b_in, b_mid.reshape(-1), last_bias.transpose(1, 0, 2).reshape(-1)]
    )
    bias = jnp.broadcast_to(bias[:, None], (bias.shape[0], 128))
    dma = pltpu.SemaphoreType.DMA
    vmem = pl.BlockSpec(memory_space=pltpu.VMEM)
    hbm = pl.BlockSpec(memory_space=pl.ANY)
    result = pl.pallas_call(
        functools.partial(kernel, n_lat, n_var, n_lev, n_row),
        out_shape=jax.ShapeDtypeStruct((n_var * n_lev * n_row, n_lon), F32),
        in_specs=[vmem] * 4 + [hbm] * 4,
        out_specs=hbm,
        scratch_shapes=[
            pltpu.VMEM((n_lon // 128, n_var * n_lev * n_row, 128), F32),
            pltpu.VMEM(w_in.shape, BF),
            pltpu.VMEM(w_mid.shape, BF),
            pltpu.VMEM(w_out.shape, BF),
            pltpu.VMEM((2, hid, feat), BF),
            pltpu.VMEM((2, feat, hid), BF),
            pltpu.VMEM((n_row, feat, n_lon), BF),
            pltpu.VMEM((2, PRE, feat, n_lon), BF),
            pltpu.VMEM((2, 2, n_row, n_lon), jnp.int32),
            pltpu.VMEM((rows, feat, n_lon), F32),
            pltpu.VMEM((rows, feat, n_lon), F32),
            pltpu.VMEM((rows, feat, n_lon), F32),
            pltpu.VMEM((rows, feat, n_lon), F32),
            pltpu.VMEM((rows, pad_lev, n_lon), F32),
            pltpu.VMEM((rows, pad_lev, n_lon), F32),
            pltpu.VMEM((2, PRE, feat, n_lon), BF),
            pltpu.VMEM((PRE, feat, n_lon), BF),
            pltpu.VMEM((hid, n_lon), BF),
            pltpu.VMEM((hid, n_lon), BF),
            pltpu.VMEM((PRE, 2, feat, n_lon), BF),
            pltpu.VMEM((n_row + 2 * POST, feat, n_lon), BF),
            dma((n_lon // 128,)),
            dma((n_lon // 128,)),
            dma((3,)),
            dma((2, 2)),
            dma((2, 2)),
            dma((2, PRE)),
            dma((2, PRE)),
            dma((PRE,)),
            dma((PRE,)),
            dma((PRE,)),
            dma((PRE,)),
            dma((POST, 2)),
            dma((2, POST)),
        ],
        compiler_params=pltpu.CompilerParams(
            collective_id=0, has_side_effects=True, vmem_limit_bytes=60 * 2**20
        ),
    )(
        region, land, table, bias, fields.reshape(n_var * n_lev * n_row, n_lon),
        w_in, w_mid, w_out,
    )
    return result.reshape(fields.shape)


def solution(mesh):
    placed = (
        P(None, "lev", ("parts", "lat"), None),
        P(("parts", "lat"), None),
        P(("parts", "lat"), None),
    ) + (P(),) * 7
    return jax.shard_map(
        functools.partial(per_device, mesh.shape["lat"]),
        mesh=mesh,
        in_specs=placed,
        out_specs=P(None, "lev", ("parts", "lat"), None),
        check_vma=False,
    )
```

profile of v0, /device:TPU:17, one launch (start us, length us, event | category | flops | bytes accessed | tf_op | source)
XLA Modules:
  0.0 110.0 jit_solution(6467789685931446353)
XLA Ops:
  0.0 0.8 reshape.21
  0.8 0.1 reshape.22
  0.9 0.8 reshape.19
  1.6 0.7 copy.20
  2.3 0.7 pad_maximum_fusion
  3.0 0.1 copy.15
  3.1 0.6 pad.8.table
  3.7 2.2 %copy.17.w_in_hbm = bf16[1024,300]{1,0:T(8,128)(2,1)} copy(bf16[1024,300]{0,1:T(8,128)(2,1)} %param.14) | data formatting | bytes 1228800 | tf_op args[4]
  6.0 1.7 %broadcast_in_dim.2.bias = f32[3392,128]{1,0:T(8,128)} broadcast(f32[3392]{0:T(1024)S(1)} %pad_maximum_fusion), dimensions={0} | broadcast | bytes 1750272 | tf_op jit(solution)/shard_map/broadcast_in_dim | solution.py:425
  7.7 98.8 %shard_map.100 = f32[1200,512]{1,0:T(8,128)} custom-call(s32[8,512]{1,0:T(8,128)} %region.1, s32[8,512]{1,0:T(8,128)} %land.1, f32[2,32,8]{2,1,0:T(8,128)} %pad.8.table, f32[3392,128]{1,0:T(8,128)} %broadcast_in_dim.2.bias, f32[1200,512]{1,0:T(8,128)} %bitcast.11, bf16[1024,300]{1,0:T(8,128)(2,1)} %copy.17.w_in_hbm, bf16[2,1024,1024]{2,1,0:T(8,128)(2,1)} %w_mid_hbm.1, ...), custom_call_target="tpu_custom_call" | custom-call | tf_op jit(solution)/shard_map/pallas_call | solution.py:429
  106.5 3.5 %copy.22 = f32[5,30,8,512]{3,2,1,0:T(8,128)} copy(f32[5,30,8,512]{3,2,1,0:T(8,128)} %bitcast.10) | data formatting | bytes 4915200
  (2 shorter events, 0.0 us)
where the time goes:
time: 110 us
  Pallas kernels  98.8 us (90%)
  local copies, waits for them, and re-layouts  10.5 us (10%)
    pallas_call x1, Pallas kernels, per_device(): pl.pallas_call(functools.partial(kernel, n_lat, n_var, n_lev, n_row), out...  98.8 us
    unnamed x3, local copies, waits for them, and re-layouts  6.42 us

commit v1 on v0

--- a/solution.py
+++ b/solution.py
@@ -23,10 +23,10 @@
 
 def kernel(
     n_lat, n_var, n_lev, n_row,
-    region, land, table, bias, fields, w_in_hbm, w_mid_hbm, w_out_hbm,
+    region, land, table, b_in, b_mid, b_out, fields, w_in_hbm, w_mid_hbm, w_out_hbm,
     out,
     split, w_in, w_mid, w_out, wi, wo,
-    sent, halo, marks, f0, f1, f2, f3, ef, nf, prof, other, h1, h2, flux_own, flux,
+    sent, halo, marks, f0, f1, f2, f3, ef, ew, nf, prof, other, h1, h2, flux_own, flux, bias,
     in_sem, out_sem, w_sem, mark_send, mark_recv, halo_send, halo_recv, prof_send, prof_recv,
     flux_send, flux_recv, edge_send, edge_recv,
 ):
@@ -35,7 +35,7 @@
     peer = 1 - lev
     has_up = lat > 0
     has_down = lat < n_lat - 1
-    pad_lev = table.shape[1]
+    pad_lev = ef.shape[1]
     feat = n_var * pad_lev
     n_lon = out.shape[1]
     hid = w_mid.shape[1]
@@ -146,9 +146,14 @@
         def _():
             row_down(k).start()
 
+    n_region, all_lev = table.shape
+    wide = jnp.concatenate([table[...], jnp.zeros((n_region, 128 - all_lev), F32)], axis=1)
+    wide = pltpu.roll(wide, (128 - lev * n_lev) % 128, 1)
+    wide = jnp.concatenate([wide] * (128 // n_region), axis=0).T[:pad_lev]
+    level_id = lax.broadcasted_iota(jnp.int32, (pad_lev, 128), 0)
+    wide = jnp.where(level_id < n_lev, wide, 0.0)
     columns = [
-        jnp.broadcast_to(table[lev, :, k : k + 1], (pad_lev, n_lon))
-        for k in range(table.shape[2])
+        jnp.broadcast_to(wide[:, k : k + 1], (pad_lev, n_lon)) for k in range(n_region)
     ]
 
     def coefficient(region_row, land_row):
@@ -166,28 +171,34 @@
 
     def faces_east(i):
         c = ef[i]
-        ef[i] = jnp.sqrt(c * pltpu.roll(c, n_lon - 1, 1))
+        east = jnp.sqrt(c * pltpu.roll(c, n_lon - 1, 1))
+        ef[i] = east
+        ew[i] = pltpu.roll(east, 1, 1)
 
     for i in range(first, last):
         faces_north(i)
 
     def step_rows(src, dst, i, store=None):
-        def body(v, carry):
-            for s in range(0, pad_lev, 16):
-                rows = pl.ds(pl.multiple_of(v * pad_lev + s, 16), 16)
+        size = 8 if store is None else 16
+        for s in range(0, pad_lev, size):
+            east = ef[i, s : s + size, :]
+            west = ew[i, s : s + size, :]
+            north = nf[i, s : s + size, :]
+            south = nf[i - 1, s : s + size, :]
+            for v in range(n_var):
+                rows = slice(v * pad_lev + s, v * pad_lev + s + size)
                 f = src[i, rows, :]
-                east = ef[i, s : s + 16, :] * (pltpu.roll(f, n_lon - 1, 1) - f)
-                zonal = east - pltpu.roll(east, 1, 1)
-                north = nf[i, s : s + 16, :] * (src[i + 1, rows, :] - f)
-                south = nf[i - 1, s : s + 16, :] * (f - src[i - 1, rows, :])
-                value = f + zonal + (north - south)
+                zonal = east * (pltpu.roll(f, n_lon - 1, 1) - f) - west * (
+                    f - pltpu.roll(f, 1, 1)
+                )
+                meridional = north * (src[i + 1, rows, :] - f) - south * (
+                    f - src[i - 1, rows, :]
+                )
+                value = f + zonal + meridional
                 if store is None:
                     dst[i, rows, :] = value
                 else:
                     store(v, s, rows, value)
-            return carry
-
-        lax.fori_loop(0, n_var, body, 0)
 
     def loop_rows(low, high, fn):
         def body(i, carry):
@@ -228,20 +239,37 @@
 
     loads[0].wait()
     loads[1].wait()
-    n_feat = w_in.shape[1]
+    n_feat = w_out.shape[0]
     for j in range(2):
-        f_id = lax.broadcasted_iota(jnp.int32, (n_feat, feat), 0)
-        c_id = lax.broadcasted_iota(jnp.int32, (n_feat, feat), 1)
-        l_id = c_id % pad_lev
-        want = (c_id // pad_lev) * (2 * n_lev) + j * n_lev + l_id
-        pick = jnp.where((f_id == want) & (l_id < n_lev), 1.0, 0.0).astype(BF)
-        wi[j] = jnp.dot(w_in[...], pick, preferred_element_type=F32).astype(BF)
         f_id = lax.broadcasted_iota(jnp.int32, (feat, n_feat), 1)
         c_id = lax.broadcasted_iota(jnp.int32, (feat, n_feat), 0)
         l_id = c_id % pad_lev
         want = (c_id // pad_lev) * (2 * n_lev) + j * n_lev + l_id
         pick = jnp.where((f_id == want) & (l_id < n_lev), 1.0, 0.0).astype(BF)
+        wi[j] = jnp.dot(pick, w_in[...], preferred_element_type=F32).T.astype(BF)
         wo[j] = jnp.dot(pick, w_out[...], preferred_element_type=F32).astype(BF)
+
+    def tall(row):
+        return jnp.broadcast_to(row, (128, 128)).T
+
+    start = (n_mid + 1) * hid
+    for m in range(0, n_feat, 128):
+        count = min(128, n_feat - m)
+        row = b_out[:, m : m + count]
+        if count < 128:
+            row = jnp.concatenate([row, jnp.zeros((1, 128 - count), F32)], axis=1)
+        bias[m : m + 128, :] = tall(row)
+    bias[start : start + 2 * feat, :] = jnp.zeros((2 * feat, 128), F32)
+    for v in range(n_var):
+        for j in range(2):
+            place = start + j * feat + v * pad_lev
+            origin = v * 2 * n_lev + j * n_lev
+            bias[place : place + n_lev, :] = bias[origin : origin + n_lev, :]
+    for m in range(0, hid, 128):
+        bias[m : m + 128, :] = tall(b_in[:, m : m + 128])
+        for layer in range(n_mid):
+            start = (layer + 1) * hid + m
+            bias[start : start + 128, :] = tall(b_mid[layer : layer + 1, m : m + 128])
     loads[2].wait()
 
     tile = 256
@@ -297,12 +325,10 @@
 
             return store
 
-        for side in range(2):
-            at = lambda k: first - p + k if side == 0 else last + p - k
-            step_rows(f0, f1, at(0))
-            step_rows(f1, f2, at(1))
-            step_rows(f2, f3, at(2))
-            step_rows(f3, None, at(3), save(side))
+        for k, (src, dst) in enumerate(((f0, f1), (f1, f2), (f2, f3), (f3, None))):
+            for side in range(2):
+                at = first - p + k if side == 0 else last + p - k
+                step_rows(src, dst, at, save(side) if dst is None else None)
         exchange = profile_copy(p)
         exchange.start()
         exchange.wait_recv()
@@ -414,26 +440,19 @@
     n_var, n_lev, n_row, n_lon = fields.shape
     hid = w_in.shape[0]
     pad_lev = -(-n_lev // 16) * 16
-    extra = pad_lev - n_lev
     feat = n_var * pad_lev
     rows = n_row + 2 * PRE
-    table = jnp.pad(coef_table.reshape(2, n_lev, -1), ((0, 0), (0, extra), (0, 0)))
-    last_bias = jnp.pad(b_out.reshape(n_var, 2, n_lev), ((0, 0), (0, 0), (0, extra)))
-    bias = jnp.concatenate(
-        [b_in, b_mid.reshape(-1), last_bias.transpose(1, 0, 2).reshape(-1)]
-    )
-    bias = jnp.broadcast_to(bias[:, None], (bias.shape[0], 128))
     dma = pltpu.SemaphoreType.DMA
     vmem = pl.BlockSpec(memory_space=pltpu.VMEM)
     hbm = pl.BlockSpec(memory_space=pl.ANY)
     result = pl.pallas_call(
         functools.partial(kernel, n_lat, n_var, n_lev, n_row),
         out_shape=jax.ShapeDtypeStruct((n_var * n_lev * n_row, n_lon), F32),
-        in_specs=[vmem] * 4 + [hbm] * 4,
+        in_specs=[vmem] * 6 + [hbm] * 4,
         out_specs=hbm,
         scratch_shapes=[
             pltpu.VMEM((n_lon // 128, n_var * n_lev * n_row, 128), F32),
-            pltpu.VMEM(w_in.shape, BF),
+            pltpu.VMEM(w_in.shape[::-1], BF),
             pltpu.VMEM(w_mid.shape, BF),
             pltpu.VMEM(w_out.shape, BF),
             pltpu.VMEM((2, hid, feat), BF),
@@ -447,12 +466,14 @@
             pltpu.VMEM((rows, feat, n_lon), F32),
             pltpu.VMEM((rows, pad_lev, n_lon), F32),
             pltpu.VMEM((rows, pad_lev, n_lon), F32),
+            pltpu.VMEM((rows, pad_lev, n_lon), F32),
             pltpu.VMEM((2, PRE, feat, n_lon), BF),
             pltpu.VMEM((PRE, feat, n_lon), BF),
             pltpu.VMEM((hid, n_lon), BF),
             pltpu.VMEM((hid, n_lon), BF),
             pltpu.VMEM((PRE, 2, feat, n_lon), BF),
             pltpu.VMEM((n_row + 2 * POST, feat, n_lon), BF),
+            pltpu.VMEM(((w_mid.shape[0] + 1) * hid + 2 * feat, 128), F32),
             dma((n_lon // 128,)),
             dma((n_lon // 128,)),
             dma((3,)),
@@ -471,8 +492,8 @@
             collective_id=0, has_side_effects=True, vmem_limit_bytes=60 * 2**20
         ),
     )(
-        region, land, table, bias, fields.reshape(n_var * n_lev * n_row, n_lon),
-        w_in, w_mid, w_out,
+        region, land, coef_table.T, b_in.reshape(1, -1), b_mid, b_out.reshape(1, -1),
+        fields.reshape(n_var * n_lev * n_row, n_lon), w_in.T, w_mid, w_out,
     )
     return result.reshape(fields.shape)
 

time: 110 us -> 71.5 us (0.65)
  Pallas kernels: 98.8 us -> 66.5 us
  local copies, waits for them, and re-layouts: 10.5 us -> 4.73 us
    pallas_call x1, Pallas kernels: 98.8 us -> 66.5 us  [per_device(): pl.pallas_call(functools.partial(kernel, n_lat, n_var, n_lev, n_row), out...]
    unnamed x3 -> x1, local copies, waits for them, and re-layouts: 6.42 us -> 3.49 us
    broadcast_in_dim x1 -> x0, local copies, waits for them, and re-layouts: 1.71 us -> none  [per_device(): bias = jnp.broadcast_to(bias[:, None], (bias.shape[0], 128))]
where the time goes in v1:
time: 71.5 us; the launch traced here: 71.2 us
  Pallas kernels  66.5 us (93%)
  local copies, waits for them, and re-layouts  4.73 us (7%)
    pallas_call x1, Pallas kernels, per_device(): pl.pallas_call(functools.partial(kernel, n_lat, n_var, n_lev, n_row), out...  66.5 us
    unnamed x1, local copies, waits for them, and re-layouts  3.49 us

profile of v1, /device:TPU:17, one launch (start us, length us, event | category | flops | bytes accessed | tf_op | source)
XLA Modules:
  0.0 71.2 jit_solution(4078594264059543137)
XLA Ops:
  0.0 1.2 %reshape.13.b_out = f32[1,300]{1,0:T(1,128)} reshape(f32[300]{0:T(512)} %param.19) | data formatting | bytes 2400 | tf_op jit(solution)/shard_map/reshape | solution.py:495
  1.2 66.5 %shard_map.100 = f32[1200,512]{1,0:T(8,128)} custom-call(s32[8,512]{1,0:T(8,128)} %region.1, s32[8,512]{1,0:T(8,128)} %land.1, f32[8,60]{1,0:T(8,128)} %bitcast.8, f32[1,1024]{1,0:T(1,128)} %bitcast.9, f32[2,1024]{1,0:T(2,128)} %b_mid.1, f32[1,300]{1,0:T(1,128)} %reshape.13.b_out, f32[1200,512]{1,0:T(8,128)} %bitcast.6, bf16[300,1024]{1,0:T(8,128)(2,1)} %bitcast.7, ...), custom_call_target="tpu_custom_call" | custom-call | tf_op jit(solution)/shard_map/pallas_call | solution.py:448
  67.7 3.5 %copy.12 = f32[5,30,8,512]{3,2,1,0:T(8,128)} copy(f32[5,30,8,512]{3,2,1,0:T(8,128)} %bitcast.5) | data formatting | bytes 4915200

commit v2 on v1

--- a/solution.py
+++ b/solution.py
@@ -94,17 +94,21 @@
             f0[PRE + r, v * pad_lev : (v + 1) * pad_lev, :] = values
             sent[r, v * pad_lev : (v + 1) * pad_lev, :] = values.astype(BF)
 
-    def row_up(k):
+    cut = feat // 2
+
+    def row_up(k, h):
+        part = pl.ds(h * cut, cut)
         return pltpu.make_async_remote_copy(
-            src_ref=sent.at[k], dst_ref=halo.at[1, k],
-            send_sem=halo_send.at[1, k], recv_sem=halo_recv.at[1, k],
+            src_ref=sent.at[k, part], dst_ref=halo.at[1, k, part],
+            send_sem=halo_send.at[1, k, h], recv_sem=halo_recv.at[1, k, h],
             device_id={"lat": lat - 1}, device_id_type=MESH,
         )
 
-    def row_down(k):
+    def row_down(k, h):
+        part = pl.ds(h * cut, cut)
         return pltpu.make_async_remote_copy(
-            src_ref=sent.at[n_row - 1 - k], dst_ref=halo.at[0, k],
-            send_sem=halo_send.at[0, k], recv_sem=halo_recv.at[0, k],
+            src_ref=sent.at[n_row - 1 - k, part], dst_ref=halo.at[0, k, part],
+            send_sem=halo_send.at[0, k, h], recv_sem=halo_recv.at[0, k, h],
             device_id={"lat": lat + 1}, device_id_type=MESH,
         )
 
@@ -126,25 +130,28 @@
     def _():
         marks_to(1, 0, region, lat - 1).start()
         marks_to(1, 1, land, lat - 1).start()
-        row_up(0).start()
+        row_up(0, 0).start()
+        row_up(0, 1).start()
 
     @pl.when(has_down)
     def _():
         marks_to(0, 0, region, lat + 1).start()
         marks_to(0, 1, land, lat + 1).start()
-        row_down(0).start()
+        row_down(0, 0).start()
+        row_down(0, 1).start()
 
     for k in range(1, PRE):
         take_row(k)
         take_row(n_row - 1 - k)
-
-        @pl.when(has_up)
-        def _():
-            row_up(k).start()
-
-        @pl.when(has_down)
-        def _():
-            row_down(k).start()
+        if k == 1:
+
+            @pl.when(has_up)
+            def _():
+                row_up(1, 0).start()
+
+            @pl.when(has_down)
+            def _():
+                row_down(1, 0).start()
 
     n_region, all_lev = table.shape
     wide = jnp.concatenate([table[...], jnp.zeros((n_region, 128 - all_lev), F32)], axis=1)
@@ -313,10 +320,12 @@
             @pl.when(exists)
             def _():
                 if side == 0:
-                    row_down(p).wait_recv()
+                    row_down(p, 0).wait_recv()
+                    row_down(p, 1).wait_recv()
                     f0[first - 1 - p] = halo[0, p].astype(F32)
                 else:
-                    row_up(p).wait_recv()
+                    row_up(p, 0).wait_recv()
+                    row_up(p, 1).wait_recv()
                     f0[last + 1 + p] = halo[1, p].astype(F32)
 
         def save(side):
@@ -331,6 +340,21 @@
                 step_rows(src, dst, at, save(side) if dst is None else None)
         exchange = profile_copy(p)
         exchange.start()
+
+        for exists, row in ((has_up, row_up), (has_down, row_down)):
+
+            @pl.when(exists & (p < PRE - 1))
+            def _():
+                row(p + 1, 1).start()
+
+            @pl.when(exists & (p < PRE - 2))
+            def _():
+                row(p + 2, 0).start()
+
+        @pl.when(has_edge & (p > half - POST))
+        def _():
+            edge_copy(p - 1, 1).start()
+
         exchange.wait_recv()
 
         for m in range(0, hid, tile):
@@ -354,12 +378,15 @@
 
         @pl.when(has_edge & (p >= half - POST))
         def _():
-            for j in range(2):
-                edge_copy(p, j).start()
+            edge_copy(p, 0).start()
 
         return carry
 
     lax.fori_loop(0, PRE, phase, 0)
+
+    @pl.when(has_edge)
+    def _():
+        edge_copy(half - 1, 1).start()
 
     for p in range(half):
         flux_copy(p).wait_recv()
@@ -417,14 +444,16 @@
         for which in range(2):
             marks_to(1, which, region, lat).wait_send()
         for k in range(PRE):
-            row_up(k).wait_send()
+            row_up(k, 0).wait_send()
+            row_up(k, 1).wait_send()
 
     @pl.when(has_down)
     def _():
         for which in range(2):
             marks_to(0, which, region, lat).wait_send()
         for k in range(PRE):
-            row_down(k).wait_send()
+            row_down(k, 0).wait_send()
+            row_down(k, 1).wait_send()
 
     @pl.when(has_edge)
     def _():
@@ -479,8 +508,8 @@
             dma((3,)),
             dma((2, 2)),
             dma((2, 2)),
-            dma((2, PRE)),
-            dma((2, PRE)),
+            dma((2, PRE, 2)),
+            dma((2, PRE, 2)),
             dma((PRE,)),
             dma((PRE,)),
             dma((PRE,)),

time: 71.5 us -> 65.7 us (0.919)
  Pallas kernels: 66.5 us -> 60.4 us
    pallas_call x1, Pallas kernels: 66.5 us -> 60.4 us  [per_device(): pl.pallas_call(functools.partial(kernel, n_lat, n_var, n_lev, n_row), out...]
where the time goes in v2:
time: 65.7 us; the launch traced here: 65.1 us
  Pallas kernels  60.4 us (92%)
  local copies, waits for them, and re-layouts  4.73 us (7%)
    pallas_call x1, Pallas kernels, per_device(): pl.pallas_call(functools.partial(kernel, n_lat, n_var, n_lev, n_row), out...  60.4 us
    unnamed x1, local copies, waits for them, and re-layouts  3.49 us

profile of v2, /device:TPU:17, one launch (start us, length us, event | category | flops | bytes accessed | tf_op | source)
XLA Modules:
  0.0 65.1 jit_solution(7248162080677310066)
XLA Ops:
  0.0 1.2 %reshape.13.b_out = f32[1,300]{1,0:T(1,128)} reshape(f32[300]{0:T(512)} %param.19) | data formatting | bytes 2400 | tf_op jit(solution)/shard_map/reshape | solution.py:524
  1.2 60.4 %shard_map.100 = f32[1200,512]{1,0:T(8,128)} custom-call(s32[8,512]{1,0:T(8,128)} %region.1, s32[8,512]{1,0:T(8,128)} %land.1, f32[8,60]{1,0:T(8,128)} %bitcast.8, f32[1,1024]{1,0:T(1,128)} %bitcast.9, f32[2,1024]{1,0:T(2,128)} %b_mid.1, f32[1,300]{1,0:T(1,128)} %reshape.13.b_out, f32[1200,512]{1,0:T(8,128)} %bitcast.6, bf16[300,1024]{1,0:T(8,128)(2,1)} %bitcast.7, ...), custom_call_target="tpu_custom_call" | custom-call | tf_op jit(solution)/shard_map/pallas_call | solution.py:477
  61.6 3.5 %copy.12 = f32[5,30,8,512]{3,2,1,0:T(8,128)} copy(f32[5,30,8,512]{3,2,1,0:T(8,128)} %bitcast.5) | data formatting | bytes 4915200
